TPU v7x, 128 devices: a whole 4x4x4 slice. The times are simulated.
128 devices in a mesh: dp: 8 (over x, core), tp: 16 (over y, z).
Axes of the slice: x: 4, y: 4, z: 4, core: 2. Of those that a mesh axis runs over, the one named last changes fastest.
Arguments:
- queries: bfloat16 [1024, 128, 576], P(('dp', 'tp')), may hold values from -10 to 10
- new_latent: bfloat16 [1024, 576], P(('dp', 'tp')), may hold values from -6 to 6
- resident: bfloat16 [768, 256, 576], P(('dp', 'tp')), may hold values from -6 to 6
- leaving: bfloat16 [256, 2, 256, 576], P(('dp', 'tp')), may hold values from -6 to 6
- res_len: int32 [768], P(('dp', 'tp')), may hold values from 1 to 256, as said below
- leave_len: int32 [128, 2], replicated, may hold values from 1 to 256, as said below
- mig_dest: int32 [128, 2], replicated, may hold values from 0 to 15, as said below
- stream: bfloat16 [1024, 7168], P(('dp', 'tp')), may hold values from -6 to 6
- dense_gain: float32 [7168], replicated, may hold values from 0.1 to 1.9
- w_gate: bfloat16 [7168, 18432], P('dp', 'tp'), may hold values from -0.0625 to 0.0625
- w_up: bfloat16 [7168, 18432], P('dp', 'tp'), may hold values from -0.0625 to 0.0625
- w_down: bfloat16 [18432, 7168], P('tp', 'dp'), may hold values from -0.046875 to 0.046875
- moe_gain: float32 [7168], replicated, may hold values from 0.1 to 1.9
- expert_gate: bfloat16 [16, 7168, 2048], P('tp', None, 'dp'), may hold values from -0.0625 to 0.0625
- expert_up: bfloat16 [16, 7168, 2048], P('tp', None, 'dp'), may hold values from -0.0625 to 0.0625
- expert_down: bfloat16 [16, 2048, 7168], P('tp', 'dp'), may hold values from -0.125 to 0.125
- expert_ids: int32 [1024, 8], P(('dp', 'tp')), may hold values from 0 to 15, all different within a row; in each aligned block of 8 rows (0 to 7, 8 to 15, ...) at most 5 rows name the same one
- gate_scores: float32 [1024, 8], P(('dp', 'tp')), may hold values from 0.05 to 1
Outputs:
- context: bfloat16 [1024, 128, 512], P(('dp', 'tp'))
- arrived: bfloat16 [256, 2, 256, 576], P(('dp', 'tp'))
- stream_out: bfloat16 [1024, 7168], P(('dp', 'tp'))
Inputs may be any that keep to these rules, and one draw needn't show every extreme that they name: `mig_dest`: each device sends its 2 leaving requests to 2 different other devices of its dp index, and every device receives exactly 2 requests. `res_len`: some request holds all 256 positions. `leave_len`: some request holds all 256 positions. `expert_ids`: among the 8 rows of one device no expert is chosen by more than 5 rows, a bound that some block reaches; a row names 8 different experts.
All inputs are finite; a program needn't handle non-finite values.
Results may differ from a plain program's by a relative error of at most 0.023.
Values may be sent and summed in bfloat16 or wider, within the bound.
A program may use at most 128 MiB of HBM per device.

v0:
```python
import jax
import jax.numpy as jnp
from jax import lax
from jax.sharding import PartitionSpec as P

VDIM = 512
QKD = 192
EPS = 1e-06
ROUTE_SCALE = 2.5


def rms_scale(rows, gain):
    values = rows.astype(jnp.float32)
    mean_square = jnp.mean(values * values, axis=-1, keepdims=True)
    return (values * lax.rsqrt(mean_square + EPS) * gain).astype(jnp.bfloat16)


def attend(queries, keys, lengths, newest):
    scale = QKD ** (-0.5)
    scores = jnp.einsum("rhl,rcl->rhc", queries, keys, preferred_element_type=jnp.float32) * scale
    positions = jnp.arange(keys.shape[1])
    valid = positions[None, None, :] < lengths[:, None, None]
    masked = jnp.where(valid, scores, -1e30)
    own_score = (
        jnp.einsum("rhl,rl->rh", queries, newest, preferred_element_type=jnp.float32) * scale
    )
    top = jnp.maximum(jnp.max(masked, axis=-1), own_score)
    expo = jnp.where(valid, jnp.exp(masked - top[..., None]), 0.0)
    own_expo = jnp.exp(own_score - top)
    total = jnp.sum(expo, axis=-1) + own_expo
    weights = (expo / total[..., None]).astype(jnp.bfloat16)
    own_weight = (own_expo / total).astype(jnp.bfloat16)
    context = jnp.einsum(
        "rhc,rcv->rhv", weights, keys[:, :, :VDIM], preferred_element_type=jnp.float32
    )
    context = context + own_weight.astype(jnp.float32)[..., None] * newest[:, None, :VDIM].astype(
        jnp.float32
    )
    return context.astype(jnp.bfloat16)


def on_device(
    queries,
    new_latent,
    resident,
    leaving,
    res_len,
    leave_len,
    mig_dest,
    stream,
    dense_gain,
    w_gate,
    w_up,
    w_down,
    moe_gain,
    expert_gate,
    expert_up,
    expert_down,
    expert_ids,
    gate_scores,
):
    tp_count = lax.axis_size("tp")
    dp_count = lax.axis_size("dp")
    tp_rank = lax.axis_index("tp")
    dp_rank = lax.axis_index("dp")
    moving = leaving.shape[0]
    device = dp_rank * tp_count + tp_rank
    peers = jnp.arange(tp_count)
    own_dest = lax.dynamic_index_in_dim(mig_dest, device, 0, keepdims=False)
    outgoing = jnp.zeros((tp_count,) + leaving.shape[1:], jnp.bfloat16)
    for slot in range(moving):
        outgoing = jnp.where(
            (peers == own_dest[slot])[:, None, None, None], leaving[slot][None], outgoing
        )
    incoming = lax.all_to_all(outgoing, "tp", split_axis=0, concat_axis=0, tiled=True)
    group_dest = lax.dynamic_slice_in_dim(mig_dest, dp_rank * tp_count, tp_count, 0)
    group_len = lax.dynamic_slice_in_dim(leave_len, dp_rank * tp_count, tp_count, 0)
    match = group_dest == tp_rank
    is_source = jnp.any(match, axis=1)
    which = jnp.sum(jnp.where(match, jnp.arange(moving)[None, :], 0), axis=1)
    order = jnp.cumsum(is_source.astype(jnp.int32)) - 1
    arrivals = []
    arrival_len = []
    for arrival in range(moving):
        pick = is_source & (order == arrival)
        source = jnp.sum(jnp.where(pick, peers, 0))
        slot = jnp.sum(jnp.where(pick, which, 0))
        arrivals.append(lax.dynamic_index_in_dim(incoming, source, 0, keepdims=False))
        source_len = lax.dynamic_index_in_dim(group_len, source, 0, keepdims=False)
        arrival_len.append(lax.dynamic_index_in_dim(source_len, slot, 0, keepdims=False))
    arrived = jnp.stack(arrivals, axis=0)
    arrived_len = jnp.stack(arrival_len, axis=0)
    stay = resident.shape[0]
    context_stay = attend(queries[:stay], resident, res_len, new_latent[:stay])
    context_moved = attend(queries[stay:], arrived[:, 0], arrived_len, new_latent[stay:])
    context = jnp.concatenate([context_stay, context_moved], axis=0)
    rows_dev = stream.shape[0]
    width = stream.shape[1]
    normed = rms_scale(stream, dense_gain)
    nearby = lax.all_gather(normed[None], "tp", axis=0, tiled=True)
    gathered = lax.all_to_all(nearby[:, None], "dp", split_axis=3, concat_axis=1, tiled=True)
    features = gathered.reshape(-1, gathered.shape[-1])
    gate_part = jnp.dot(features, w_gate, preferred_element_type=jnp.float32)
    up_part = jnp.dot(features, w_up, preferred_element_type=jnp.float32)
    gate, up = (
        lax.psum(gate_part.astype(jnp.bfloat16), "dp").astype(jnp.float32),
        lax.psum(up_part.astype(jnp.bfloat16), "dp").astype(jnp.float32),
    )
    hidden_all = (jax.nn.silu(gate) * up).astype(jnp.bfloat16)
    block = hidden_all
    ffn_share = lax.psum_scatter(
        jnp.dot(block, w_down, preferred_element_type=jnp.float32).astype(jnp.bfloat16),
        "tp",
        scatter_dimension=0,
        tiled=True,
    ).astype(jnp.float32)
    ffn_rows = lax.all_to_all(
        ffn_share.reshape(dp_count, rows_dev, ffn_share.shape[-1]).astype(jnp.bfloat16),
        "dp",
        split_axis=0,
        concat_axis=2,
        tiled=True,
    ).astype(jnp.float32)
    middle = (stream.astype(jnp.float32) + ffn_rows[0]).astype(jnp.bfloat16)
    mixed = rms_scale(middle, moe_gain)
    experts = expert_gate.shape[0] * tp_count
    top_count = expert_ids.shape[1]
    capacity = min(rows_dev, rows_dev * top_count // experts + 1)
    hits = (expert_ids[:, :, None] == jnp.arange(experts)[None, None, :]).astype(jnp.int32)
    row_hits = jnp.sum(hits, axis=1)
    before = jnp.cumsum(row_hits, axis=0) - row_hits
    slot_of = jnp.sum(hits * before[:, None, :], axis=2)
    target = expert_ids * capacity + slot_of
    placed = jnp.any(target[:, :, None] == jnp.arange(experts * capacity)[None, None, :], axis=1)
    outgoing_rows = jnp.dot(
        placed.T.astype(jnp.bfloat16), mixed, preferred_element_type=jnp.float32
    )
    outgoing_rows = outgoing_rows.astype(jnp.bfloat16).reshape(experts, capacity, width)
    received = lax.all_to_all(outgoing_rows, "tp", split_axis=0, concat_axis=0, tiled=True)
    pooled = lax.all_gather(received, "dp", axis=0, tiled=True)
    flat = pooled.reshape(-1, width)
    block = flat
    gate = jnp.dot(block, expert_gate[0], preferred_element_type=jnp.float32)
    up = jnp.dot(block, expert_up[0], preferred_element_type=jnp.float32)
    inner = (jax.nn.silu(gate) * up).astype(jnp.bfloat16)
    summed = lax.psum_scatter(
        jnp.dot(inner, expert_down[0], preferred_element_type=jnp.float32).astype(jnp.bfloat16),
        "dp",
        scatter_dimension=0,
        tiled=True,
    )
    results = summed.reshape(received.shape)
    returned = lax.all_to_all(results, "tp", split_axis=0, concat_axis=0, tiled=True)
    flat_back = returned.reshape(experts * capacity, width)
    picked = jnp.take(flat_back, target.reshape(-1), axis=0).reshape(rows_dev, top_count, width)
    shares = gate_scores / jnp.sum(gate_scores, axis=1, keepdims=True) * ROUTE_SCALE
    routed = jnp.einsum("rk,rkd->rd", shares, picked.astype(jnp.float32))
    stream_out = (middle.astype(jnp.float32) + routed).astype(jnp.bfloat16)
    return (context, arrived, stream_out)


def solution(mesh):
    placed = (
        P(("dp", "tp"), None, None),
        P(("dp", "tp"), None),
        P(("dp", "tp"), None, None),
        P(("dp", "tp"), None, None, None),
        P(("dp", "tp")),
        P(),
        P(),
        P(("dp", "tp"), None),
        P(),
        P("dp", "tp"),
        P("dp", "tp"),
        P("tp", "dp"),
        P(),
        P("tp", None, "dp"),
        P("tp", None, "dp"),
        P("tp", "dp", None),
        P(("dp", "tp"), None),
        P(("dp", "tp"), None),
    )
    return jax.shard_map(
        on_device,
        mesh=mesh,
        in_specs=placed,
        out_specs=(
            P(("dp", "tp"), None, None),
            P(("dp", "tp"), None, None, None),
            P(("dp", "tp"), None),
        ),
        check_vma=False,
    )
```

profile of v0, /device:TPU:0, one launch (start us, length us, event | category | flops | bytes accessed | tf_op | source)
XLA Modules:
  0.0 688.6 jit_solution(10923640459823760998)
XLA Ops:
  7.2 1.2 fusion.49
  8.4 1.6 fusion.51
  10.2 47.7 %all-gather.6.cloned.1.call-done = bf16[128,7168]{1,0:T(8,128)(2,1)} async-done(((bf16[8,7168]{1,0:T(8,128)(2,1)}), bf16[128,7168]{1,0:T(8,128)(2,1)}) %all-gather.6.cloned.1.call-update) | async-done | bytes 1835024 | tf_op jit(solution)/shard_map/all_gather | solution.py:100
  57.8 13.7 %copy.81 = bf16[16,1,8,7168]{0,2,1,3:T(8,128)(2,1)} copy(bf16[16,1,8,7168]{3,2,0,1:T(8,128)(2,1)} %bitcast.99) | data formatting | bytes 3670016 | tf_op jit(solution)/shard_map/broadcast_in_dim | solution.py:101
  71.6 17.3 %reshape.231 = bf16[8,2,57344]{2,1,0:T(2,128)(2,1)} reshape(bf16[7168,1,8,16]{3,2,1,0:T(8,128)(2,1)} %bitcast.94) | data formatting | bytes 3670016
  88.8 28.8 %all_to_all.39 = bf16[8,2,57344]{2,1,0:T(2,128)(2,1)} all-to-all(bf16[8,2,57344]{2,1,0:T(2,128)(2,1)} %reshape.231), channel_id=1, replica_groups=mesh['dp'=8,'tp'=16] {'dp'}, dimensions={0} | all-to-all | bytes 3670016 | tf_op jit(solution)/shard_map/all_to_all | solution.py:101
  117.6 12.5 %reshape.232 = bf16[7168,1,8,16]{3,2,1,0:T(8,128)(2,1)} reshape(bf16[8,2,57344]{2,1,0:T(2,128)(2,1)} %all_to_all.39) | data formatting | bytes 3670016
  130.1 13.8 %copy.95 = bf16[16,1,8,8,896]{4,3,2,0,1:T(8,128)(2,1)} copy(bf16[16,1,8,8,896]{0,2,4,3,1:T(8,128)(2,1)} %bitcast.95) | data formatting | bytes 3670016 | tf_op jit(solution)/shard_map/all_to_all | solution.py:101
  143.9 1.8 copy.83
  145.8 4.1 convolution_convert_fusion.2
  149.8 4.1 convolution_convert_fusion.3
  154.0 71.9 %all-reduce.3.cloned.1.call-done = (bf16[1024,1152]{1,0:T(8,128)(2,1)}, bf16[1024,1152]{1,0:T(8,128)(2,1)}) async-done(((bf16[1024,1152]{1,0:T(8,128)(2,1)}, bf16[1024,1152]{1,0:T(8,128)(2,1)}), (bf16[1024,1152]{1,0:T(8,128)(2,1)}, bf16[1024,1152]{1,0:T(8,128)(2,1)})) %all-reduce.3.cloned.1.call-update) | async-done | bytes 4718608 | tf_op jit(solution)/shard_map/psum | solution.py:107
  225.9 7.3 %fusion.12 = bf16[1024,896]{1,0:T(8,128)(2,1)} fusion(bf16[1152,896]{1,0:T(8,128)(2,1)} %param.29, bf16[1024,1152]{1,0:T(8,128)(2,1)} %get-tuple-element.30, bf16[1024,1152]{1,0:T(8,128)(2,1)} %get-tuple-element.31), kind=kOutput, calls=%fused_computation.19 | convolution fusion | flops 2124283904 | bytes 8617984 | tf_op jit(solution)/shard_map/dot_general | solution.py:112
  233.3 0.1 convert_reduce_fusion
  233.4 0.3 select_reduce_fusion
  233.7 75.1 %reduce-scatter.3.cloned.1.call-done = bf16[64,896]{1,0:T(8,128)(2,1)} async-done(((bf16[1024,896]{1,0:T(8,128)(2,1)}), bf16[64,896]{1,0:T(8,128)(2,1)}) %reduce-scatter.3.cloned.1.call-update) | async-done | bytes 114704 | tf_op jit(solution)/shard_map/reduce_scatter | solution.py:111
  308.7 4.3 all-to-all-start.2
  313.0 0.2 all-gather.4.cloned.1.call-start
  313.2 0.1 fusion.65
  313.3 5.6 all-to-all-done.2
  318.9 0.2 fusion.53
  319.1 0.5 convolution_convert_fusion.1
  319.7 0.6 reshape.205
  320.2 29.9 %all_to_all.40 = bf16[16,5,7168]{2,1,0:T(8,128)(2,1)S(1)} all-to-all(bf16[16,5,7168]{2,1,0:T(8,128)(2,1)S(1)} %reshape.205), channel_id=1, replica_groups=mesh['dp'=8,'tp'=16] {'tp'}, dimensions={0} | all-to-all | bytes 2293760 | tf_op jit(solution)/shard_map/all_to_all | solution.py:139
  350.2 1.8 copy.84
  352.0 49.3 %all-gather.4.cloned.1.call-done = bf16[128,5,7168]{2,0,1:T(8,128)(2,1)} async-done(((bf16[16,5,7168]{2,0,1:T(8,128)(2,1)}), bf16[128,5,7168]{2,0,1:T(8,128)(2,1)}) %all-gather.4.cloned.1.call-update) | async-done | bytes 9175056 | tf_op jit(solution)/shard_map/all_gather | solution.py:140
  401.3 14.0 %copy.85 = bf16[128,5,7168]{2,1,0:T(8,128)(2,1)} copy(bf16[128,5,7168]{2,0,1:T(8,128)(2,1)} %all-gather.4.cloned.1.call-done) | data formatting | bytes 18350080 | tf_op jit(solution)/shard_map/all_gather | solution.py:140
  415.3 15.1 %reshape.206 = bf16[640,7168]{1,0:T(8,128)(2,1)} reshape(bf16[128,5,7168]{2,1,0:T(8,128)(2,1)} %copy.85) | data formatting | bytes 18350080 | tf_op jit(solution)/shard_map/reshape | solution.py:141
  430.4 7.2 %fusion.8 = f32[640,256]{1,0:T(8,128)S(1)} fusion(bf16[640,7168]{1,0:T(8,128)(2,1)} %reshape.206, bf16[1,7168,256]{2,1,0:T(8,128)(2,1)} %param.31), kind=kOutput, calls=%fused_computation.16 | convolution fusion | flops 2348810240 | bytes 13500416 | tf_op jit(solution)/shard_map/dot_general | solution.py:143
  437.6 18.9 %convolution_convert_fusion = bf16[640,7168]{1,0:T(8,128)(2,1)} fusion(bf16[1,256,7168]{2,1,0:T(8,128)(2,1)} %param.33, bf16[640,7168]{1,0:T(8,128)(2,1)} %reshape.206, bf16[1,7168,256]{2,1,0:T(8,128)(2,1)} %param.32, f32[640,256]{1,0:T(8,128)S(1)} %fusion.8), kind=kOutput, calls=%fused_computation.1 | convolution fusion | flops 4703191040 | bytes 26345472 | tf_op jit(solution)/shard_map/dot_general | solution.py:147
  456.5 0.6 copy-done.13
  457.2 0.5 fusion.86
  457.7 1.3 iota_compare_fusion.4
  459.1 0.1 slice_bitcast_fusion.1
  459.1 4.9 select_select_fusion
  464.1 7.2 %all-to-all-start = ((bf16[16,2,256,576]{2,3,1,0:T(8,128)(2,1)}), bf16[16,2,256,576]{2,3,1,0:T(8,128)(2,1)}, u32[]{:S(2)}, u32[]{:S(2)}) async-start(bf16[16,2,256,576]{2,3,1,0:T(8,128)(2,1)} %select_select_fusion), calls=%async_computation | async-start | bytes 18874368 | tf_op jit(solution)/shard_map/all_to_all | solution.py:75
  471.2 0.1 fusion.84
  471.4 0.1 copy.76
  471.5 0.1 compare_reduce_fusion
  471.6 0.7 select_reduce_fusion.4
  477.3 0.1 reshape.209
  479.9 0.1 reduce_sum.116
  480.0 0.6 fusion.85
  480.6 1.4 pad_add_fusion
  482.1 0.2 fusion.66
  482.3 2.2 fusion.88
  484.6 0.3 fusion.38
  485.1 0.2 fusion.68
  485.3 1.6 add_convert_fusion
  486.9 148.7 %all-to-all-done = bf16[16,2,256,576]{2,3,1,0:T(8,128)(2,1)} async-done(((bf16[16,2,256,576]{2,3,1,0:T(8,128)(2,1)}), bf16[16,2,256,576]{2,3,1,0:T(8,128)(2,1)}, u32[]{:S(2)}, u32[]{:S(2)}) %all-to-all-start) | async-done | bytes 9437216 | tf_op jit(solution)/shard_map/all_to_all | solution.py:75
  635.6 1.3 dynamic-slice_bitcast_fusion
  637.0 1.1 fusion.87
  638.1 2.6 reshape.207
  640.7 10.5 %all-to-all-start.4 = ((bf16[16,5,7168]{2,1,0:T(8,128)(2,1)}), bf16[16,5,7168]{2,1,0:T(8,128)(2,1)S(1)}, u32[]{:S(2)}, u32[]{:S(2)}) async-start(bf16[16,5,7168]{2,1,0:T(8,128)(2,1)} %reshape.207), calls=%async_computation.6 | async-start | bytes 3670016 | tf_op jit(solution)/shard_map/all_to_all | solution.py:153
  651.2 0.1 pad_maximum_fusion
  651.3 1.1 copy.86
  652.4 0.1 fusion.57
  652.6 0.5 fusion.28
  653.1 1.1 pad_maximum_fusion.1
  654.1 23.0 %all-to-all-done.4 = bf16[16,5,7168]{2,1,0:T(8,128)(2,1)S(1)} async-done(((bf16[16,5,7168]{2,1,0:T(8,128)(2,1)}), bf16[16,5,7168]{2,1,0:T(8,128)(2,1)S(1)}, u32[]{:S(2)}, u32[]{:S(2)}) %all-to-all-start.4) | async-done | bytes 1146912 | tf_op jit(solution)/shard_map/all_to_all | solution.py:153
  677.1 0.6 reshape.208
  677.7 2.1 gather_fusion
  679.7 1.6 fusion.31
  681.4 0.7 fusion.56
  (69 shorter events, 0.9 us)
Async XLA Ops:
  7.2 138.6 %copy-start = (bf16[896,1152]{1,0:T(8,128)(2,1)S(1)}, bf16[896,1152]{1,0:T(8,128)(2,1)}, u32[]{:S(2)}) copy-start(bf16[896,1152]{1,0:T(8,128)(2,1)} %param.28) | copy-start | bytes 6193156
  7.2 50.6 %all-gather.6.cloned.1.call-start = ((), (), s32[]{:S(2)}) async-start(), calls=%async_computation.10 | async-start | bytes 1949696 | tf_op jit(solution)/shard_map/all_gather | solution.py:100
  10.1 215.8 %all-reduce.3.cloned.1.call-start = ((), (), s32[]{:S(2)}) async-start(), calls=%async_computation.11 | async-start | bytes 9437184 | tf_op jit(solution)/shard_map/psum | solution.py:107
  145.7 4.1 copy-start.16
  154.0 154.8 %reduce-scatter.3.cloned.1.call-start = ((), (), s32[]{:S(2)}) async-start(), calls=%async_computation.7 | async-start | bytes 1949696 | tf_op jit(solution)/shard_map/reduce_scatter | solution.py:111
  225.9 7.4 %copy-start.10 = (s32[8,8]{1,0:T(8,128)S(1)}, s32[8,8]{1,0:T(8,128)}, u32[]{:S(2)}) copy-start(s32[8,8]{1,0:T(8,128)} %param.34) | copy-start | bytes 772
  233.2 85.7 %copy-start.4 = (bf16[8,7168]{1,0:T(8,128)(2,1)S(1)}, bf16[8,7168]{1,0:T(8,128)(2,1)}, u32[]{:S(2)}) copy-start(bf16[8,7168]{1,0:T(8,128)(2,1)} %param.25) | copy-start | bytes 344068
  233.2 85.9 %copy-start.11 = (f32[7168]{0:T(1024)S(1)}, f32[7168]{0:T(1024)}, u32[]{:S(2)}) copy-start(f32[7168]{0:T(1024)} %param.30) | copy-start | bytes 86020
  308.7 10.2 %all-to-all-start.2 = ((bf16[8,8,896]{2,1,0:T(8,128)(2,1)}), bf16[8,8,896]{2,1,0:T(8,128)(2,1)S(1)}, u32[]{:S(2)}, u32[]{:S(2)}) async-start(bf16[8,8,896]{2,1,0:T(8,128)(2,1)} %bitcast.101), calls=%async_computation.3 | async-start | bytes 229376 | tf_op jit(solution)/shard_map/all_to_all | solution.py:117
  313.0 88.3 %all-gather.4.cloned.1.call-start = ((), (), s32[]{:S(2)}) async-start(), calls=%async_computation.8 | async-start | bytes 10321920 | tf_op jit(solution)/shard_map/all_gather | solution.py:140
  351.9 286.2 %reduce-scatter.5.cloned.1.call-start = ((), (), s32[]{:S(2)}) async-start(), calls=%async_computation.9 | async-start | bytes 10321920 | tf_op jit(solution)/shard_map/reduce_scatter | solution.py:146
  456.5 0.7 copy-start.13
  456.5 2.6 copy-start.3
  464.0 15.9 %copy-start.12 = (f32[8,8]{1,0:T(8,128)S(1)}, f32[8,8]{1,0:T(8,128)}, u32[]{:S(2)}) copy-start(f32[8,8]{1,0:T(8,128)} %param.35) | copy-start | bytes 772
  464.0 16.0 %copy-start.14 = (s32[128,2]{0,1:T(2,128)S(1)}, s32[128,2]{0,1:T(2,128)}, u32[]{:S(2)}) copy-start(s32[128,2]{0,1:T(2,128)} %param.23) | copy-start | bytes 3076
  464.0 18.0 %copy-start.15 = (s32[6]{0:T(128)S(1)}, s32[6]{0:T(128)}, u32[]{:S(2)}) copy-start(s32[6]{0:T(128)} %param.22) | copy-start | bytes 76
  464.0 18.1 %copy-start.9 = (bf16[8,576]{1,0:T(8,128)(2,1)S(1)}, bf16[8,576]{1,0:T(8,128)(2,1)}, u32[]{:S(2)}) copy-start(bf16[8,576]{1,0:T(8,128)(2,1)} %param.19) | copy-start | bytes 27652
  464.1 18.1 %copy-start.2 = (bf16[8,128,576]{1,2,0:T(8,128)(2,1)S(1)}, bf16[8,128,576]{1,2,0:T(8,128)(2,1)}, u32[]{:S(2)}) copy-start(bf16[8,128,576]{1,2,0:T(8,128)(2,1)} %param.18) | copy-start | bytes 3538948
  464.1 171.5 %all-to-all-start = ((bf16[16,2,256,576]{2,3,1,0:T(8,128)(2,1)}), bf16[16,2,256,576]{2,3,1,0:T(8,128)(2,1)}, u32[]{:S(2)}, u32[]{:S(2)}) async-start(bf16[16,2,256,576]{2,3,1,0:T(8,128)(2,1)} %select_select_fusion), calls=%async_computation | async-start | bytes 18874368 | tf_op jit(solution)/shard_map/all_to_all | solution.py:75
  482.3 2.9 copy-start.17
  637.0 3.7 copy-start.6
  640.7 36.4 %all-to-all-start.4 = ((bf16[16,5,7168]{2,1,0:T(8,128)(2,1)}), bf16[16,5,7168]{2,1,0:T(8,128)(2,1)S(1)}, u32[]{:S(2)}, u32[]{:S(2)}) async-start(bf16[16,5,7168]{2,1,0:T(8,128)(2,1)} %reshape.207), calls=%async_computation.6 | async-start | bytes 3670016 | tf_op jit(solution)/shard_map/all_to_all | solution.py:153
  651.2 1.2 copy-start.8
  651.2 1.4 copy-start.7
  651.3 1.8 copy-start.5
  677.7 4.4 copy-start.1
Sparse Core Ops, SparseCore 0:
  10.7 47.0 all-gather.5
  154.1 71.7 all-reduce.2
  233.4 75.3 reduce-scatter.2
  352.1 49.2 all-gather.3
  456.6 56.3 reduce-scatter.4
where the time goes:
time: 690 us; the launch traced here: 689 us
  waiting for transfers between devices  421 us (61%)
  local copies, waits for them, and re-layouts  100 us (14%)
  blocking collectives  58.7 us (9%)
  matrix products  49.5 us (7%)
  starting transfers between devices  22.3 us (3%)
  between operations  21.7 us (3%)
  other arithmetic  14.9 us (2%)
    all_to_all x1, waiting for transfers between devices, on_device(): lax.all_to_all(outgoing, 'tp', split_axis=0, concat_axis=0, tiled=True)  149 us
    reduce_scatter x1, waiting for transfers between devices, on_device(): lax.psum_scatter(jnp.dot(block, w_down, preferred_element_type=jnp.float3...  75.1 us
    psum x1, waiting for transfers between devices, on_device(): lax.psum(up_part.astype(jnp.bfloat16), 'dp').astype(jnp.float32)  71.9 us
    all_gather x1, waiting for transfers between devices, on_device(): pooled = lax.all_gather(received, 'dp', axis=0, tiled=True)  49.3 us
    all_gather x1, waiting for transfers between devices, on_device(): nearby = lax.all_gather(normed[None], 'tp', axis=0, tiled=True)  47.7 us
    unnamed x40, local copies, waits for them, and re-layouts  32.9 us
    all_to_all x1, blocking collectives, on_device(): lax.all_to_all(outgoing_rows, 'tp', split_axis=0, concat_axis=0, tiled=True)  29.9 us
    all_to_all x1, blocking collectives, on_device(): lax.all_to_all(nearby[:, None], 'dp', split_axis=3, concat_axis=1, tiled=...  28.8 us
  transfers between devices with their start and end apart: 8, of which 7 were waited for; matrix products, arithmetic and copies ran while one was open for 3% of the time, Pallas kernels for 0%

commit v1 on v0

--- a/solution.py
+++ b/solution.py
@@ -97,7 +97,9 @@
     rows_dev = stream.shape[0]
     width = stream.shape[1]
     normed = rms_scale(stream, dense_gain)
-    nearby = lax.all_gather(normed[None], "tp", axis=0, tiled=True)
+    x = normed[None]
+    stack = jnp.stack([x] * lax.axis_size("tp"))
+    nearby = jnp.concatenate(lax.all_to_all(stack, "tp", 0, 0), axis=0)
     gathered = lax.all_to_all(nearby[:, None], "dp", split_axis=3, concat_axis=1, tiled=True)
     features = gathered.reshape(-1, gathered.shape[-1])
     gate_part = jnp.dot(features, w_gate, preferred_element_type=jnp.float32)

time: 690 us -> 675 us (0.978)
  waiting for transfers between devices: 421 us -> 373 us
  blocking collectives: 58.7 us -> 92.2 us
    all_gather x1 -> x0, waiting for transfers between devices: 47.7 us -> none  [on_device(): nearby = lax.all_gather(normed[None], 'tp', axis=0, tiled=True)]
    all_to_all x0 -> x1, blocking collectives: none -> 33.4 us  [on_device(): nearby = jnp.concatenate(lax.all_to_all(stack, 'tp', 0, 0), axis=0)]
    all_to_all x0 -> x1, local copies, waits for them, and re-layouts: none -> 13.7 us  [on_device(): nearby = jnp.concatenate(lax.all_to_all(stack, 'tp', 0, 0), axis=0)]
    broadcast_in_dim x1 -> x0, local copies, waits for them, and re-layouts: 13.7 us -> none  [on_device(): nearby[:, None]]
  transfers between devices with their start and end apart: 8 -> 7, of which waited for: 7 -> 6; matrix products, arithmetic and copies ran while one was open for 3% -> 3% of each run, Pallas kernels for 0% -> 0%
where the time goes in v1:
time: 675 us; the launch traced here: 673 us
  waiting for transfers between devices  373 us (55%)
  local copies, waits for them, and re-layouts  100 us (15%)
  blocking collectives  92.2 us (14%)
  matrix products  49.5 us (7%)
  starting transfers between devices  22.1 us (3%)
  between operations  21.7 us (3%)
  other arithmetic  14.2 us (2%)
    all_to_all x1, waiting for transfers between devices, on_device(): lax.all_to_all(outgoing, 'tp', split_axis=0, concat_axis=0, tiled=True)  149 us
    reduce_scatter x1, waiting for transfers between devices, on_device(): lax.psum_scatter(jnp.dot(block, w_down, preferred_element_type=jnp.float3...  75.1 us
    psum x1, waiting for transfers between devices, on_device(): lax.psum(up_part.astype(jnp.bfloat16), 'dp').astype(jnp.float32)  70.8 us
    all_gather x1, waiting for transfers between devices, on_device(): pooled = lax.all_gather(received, 'dp', axis=0, tiled=True)  49.3 us
    all_to_all x1, blocking collectives, on_device(): nearby = jnp.concatenate(lax.all_to_all(stack, 'tp', 0, 0), axis=0)  33.4 us
    unnamed x40, local copies, waits for them, and re-layouts  32.9 us
    all_to_all x1, blocking collectives, on_device(): lax.all_to_all(outgoing_rows, 'tp', split_axis=0, concat_axis=0, tiled=True)  29.9 us
    all_to_all x1, blocking collectives, on_device(): lax.all_to_all(nearby[:, None], 'dp', split_axis=3, concat_axis=1, tiled=...  28.8 us
  transfers between devices with their start and end apart: 7, of which 6 were waited for; matrix products, arithmetic and copies ran while one was open for 3% of the time, Pallas kernels for 0%

profile of v1, /device:TPU:0, one launch (start us, length us, event | category | flops | bytes accessed | tf_op | source)
XLA Modules:
  0.0 672.8 jit_solution(1972821689849838458)
XLA Ops:
  7.2 1.2 fusion.49
  8.4 1.0 fusion.51
  9.4 0.2 stack.15
  9.6 33.4 %all_to_all.44 = bf16[16,1,8,7168]{3,2,1,0:T(8,128)(2,1)} all-to-all(bf16[16,1,8,7168]{3,2,1,0:T(8,128)(2,1)S(1)} %stack.15), channel_id=1, replica_groups=mesh['dp'=8,'tp'=16] {'tp'}, dimensions={0} | all-to-all | bytes 3670016 | tf_op jit(solution)/shard_map/all_to_all | solution.py:102
  43.1 13.7 %copy.71 = bf16[16,1,8,7168]{0,2,1,3:T(8,128)(2,1)} copy(bf16[16,1,8,7168]{3,2,1,0:T(8,128)(2,1)} %all_to_all.44) | data formatting | bytes 3670016 | tf_op jit(solution)/shard_map/all_to_all | solution.py:102
  56.8 17.3 %reshape.231 = bf16[8,2,57344]{2,1,0:T(2,128)(2,1)} reshape(bf16[7168,1,8,16]{3,2,1,0:T(8,128)(2,1)} %bitcast.93) | data formatting | bytes 3670016
  74.1 28.8 %all_to_all.45 = bf16[8,2,57344]{2,1,0:T(2,128)(2,1)} all-to-all(bf16[8,2,57344]{2,1,0:T(2,128)(2,1)} %reshape.231), channel_id=1, replica_groups=mesh['dp'=8,'tp'=16] {'dp'}, dimensions={0} | all-to-all | bytes 3670016 | tf_op jit(solution)/shard_map/all_to_all | solution.py:103
  102.9 12.5 %reshape.232 = bf16[7168,1,8,16]{3,2,1,0:T(8,128)(2,1)} reshape(bf16[8,2,57344]{2,1,0:T(2,128)(2,1)} %all_to_all.45) | data formatting | bytes 3670016
  115.4 13.8 %copy.85 = bf16[16,1,8,8,896]{4,3,2,0,1:T(8,128)(2,1)} copy(bf16[16,1,8,8,896]{0,2,4,3,1:T(8,128)(2,1)} %bitcast.94) | data formatting | bytes 3670016 | tf_op jit(solution)/shard_map/all_to_all | solution.py:103
  129.2 1.8 copy.73
  131.0 4.1 convolution_convert_fusion.2
  135.1 4.1 convolution_convert_fusion.3
  139.3 70.8 %all-reduce.3.cloned.1.call-done = (bf16[1024,1152]{1,0:T(8,128)(2,1)}, bf16[1024,1152]{1,0:T(8,128)(2,1)}) async-done(((bf16[1024,1152]{1,0:T(8,128)(2,1)}, bf16[1024,1152]{1,0:T(8,128)(2,1)}), (bf16[1024,1152]{1,0:T(8,128)(2,1)}, bf16[1024,1152]{1,0:T(8,128)(2,1)})) %all-reduce.3.cloned.1.call-update) | async-done | bytes 4718608 | tf_op jit(solution)/shard_map/psum | solution.py:109
  210.1 7.3 %fusion.12 = bf16[1024,896]{1,0:T(8,128)(2,1)} fusion(bf16[1152,896]{1,0:T(8,128)(2,1)} %param.29, bf16[1024,1152]{1,0:T(8,128)(2,1)} %get-tuple-element.27, bf16[1024,1152]{1,0:T(8,128)(2,1)} %get-tuple-element.28), kind=kOutput, calls=%fused_computation.19 | convolution fusion | flops 2124283904 | bytes 8617984 | tf_op jit(solution)/shard_map/dot_general | solution.py:114
  217.4 0.1 convert_reduce_fusion
  217.6 0.3 select_reduce_fusion
  217.9 75.1 %reduce-scatter.3.cloned.1.call-done = bf16[64,896]{1,0:T(8,128)(2,1)} async-done(((bf16[1024,896]{1,0:T(8,128)(2,1)}), bf16[64,896]{1,0:T(8,128)(2,1)}) %reduce-scatter.3.cloned.1.call-update) | async-done | bytes 114704 | tf_op jit(solution)/shard_map/reduce_scatter | solution.py:113
  292.9 4.3 all-to-all-start.3
  297.2 0.1 fusion.65
  297.3 5.8 all-to-all-done.3
  303.1 0.2 fusion.53
  303.3 0.5 convolution_convert_fusion.1
  303.8 0.6 reshape.207
  304.4 29.9 %all_to_all.46 = bf16[16,5,7168]{2,1,0:T(8,128)(2,1)S(1)} all-to-all(bf16[16,5,7168]{2,1,0:T(8,128)(2,1)S(1)} %reshape.207), channel_id=1, replica_groups=mesh['dp'=8,'tp'=16] {'tp'}, dimensions={0} | all-to-all | bytes 2293760 | tf_op jit(solution)/shard_map/all_to_all | solution.py:141
  334.3 1.8 copy.74
  336.2 49.3 %all-gather.2.cloned.1.call-done = bf16[128,5,7168]{2,0,1:T(8,128)(2,1)} async-done(((bf16[16,5,7168]{2,0,1:T(8,128)(2,1)}), bf16[128,5,7168]{2,0,1:T(8,128)(2,1)}) %all-gather.2.cloned.1.call-update) | async-done | bytes 9175056 | tf_op jit(solution)/shard_map/all_gather | solution.py:142
  385.5 14.0 %copy.75 = bf16[128,5,7168]{2,1,0:T(8,128)(2,1)} copy(bf16[128,5,7168]{2,0,1:T(8,128)(2,1)} %all-gather.2.cloned.1.call-done) | data formatting | bytes 18350080 | tf_op jit(solution)/shard_map/all_gather | solution.py:142
  399.5 15.1 %reshape.208 = bf16[640,7168]{1,0:T(8,128)(2,1)} reshape(bf16[128,5,7168]{2,1,0:T(8,128)(2,1)} %copy.75) | data formatting | bytes 18350080 | tf_op jit(solution)/shard_map/reshape | solution.py:143
  414.6 7.2 %fusion.8 = f32[640,256]{1,0:T(8,128)S(1)} fusion(bf16[640,7168]{1,0:T(8,128)(2,1)} %reshape.208, bf16[1,7168,256]{2,1,0:T(8,128)(2,1)} %param.31), kind=kOutput, calls=%fused_computation.16 | convolution fusion | flops 2348810240 | bytes 13500416 | tf_op jit(solution)/shard_map/dot_general | solution.py:145
  421.8 18.9 %convolution_convert_fusion = bf16[640,7168]{1,0:T(8,128)(2,1)} fusion(bf16[1,256,7168]{2,1,0:T(8,128)(2,1)} %param.33, bf16[640,7168]{1,0:T(8,128)(2,1)} %reshape.208, bf16[1,7168,256]{2,1,0:T(8,128)(2,1)} %param.32, f32[640,256]{1,0:T(8,128)S(1)} %fusion.8), kind=kOutput, calls=%fused_computation.1 | convolution fusion | flops 4703191040 | bytes 26345472 | tf_op jit(solution)/shard_map/dot_general | solution.py:149
  440.7 0.6 copy-done.13
  441.4 0.5 fusion.86
  441.9 1.3 iota_compare_fusion.4
  443.2 0.1 slice_bitcast_fusion.1
  443.3 4.9 select_select_fusion
  448.2 7.2 %all-to-all-start = ((bf16[16,2,256,576]{2,3,1,0:T(8,128)(2,1)}), bf16[16,2,256,576]{2,3,1,0:T(8,128)(2,1)}, u32[]{:S(2)}, u32[]{:S(2)}) async-start(bf16[16,2,256,576]{2,3,1,0:T(8,128)(2,1)} %select_select_fusion), calls=%async_computation | async-start | bytes 18874368 | tf_op jit(solution)/shard_map/all_to_all | solution.py:75
  455.4 0.1 fusion.84
  455.5 0.1 copy.66
  455.7 0.1 compare_reduce_fusion
  455.8 0.7 select_reduce_fusion.4
  461.5 0.1 reshape.211
  464.1 0.1 reduce_sum.116
  464.2 0.6 fusion.85
  464.8 1.4 pad_add_fusion
  466.3 0.2 fusion.66
  466.5 2.2 fusion.88
  468.8 0.3 fusion.38
  469.3 0.2 fusion.68
  469.5 1.6 add_convert_fusion
  471.1 148.7 %all-to-all-done = bf16[16,2,256,576]{2,3,1,0:T(8,128)(2,1)} async-done(((bf16[16,2,256,576]{2,3,1,0:T(8,128)(2,1)}), bf16[16,2,256,576]{2,3,1,0:T(8,128)(2,1)}, u32[]{:S(2)}, u32[]{:S(2)}) %all-to-all-start) | async-done | bytes 9437216 | tf_op jit(solution)/shard_map/all_to_all | solution.py:75
  619.8 1.3 dynamic-slice_bitcast_fusion
  621.2 1.1 fusion.87
  622.3 2.6 reshape.209
  624.9 10.5 %all-to-all-start.5 = ((bf16[16,5,7168]{2,1,0:T(8,128)(2,1)}), bf16[16,5,7168]{2,1,0:T(8,128)(2,1)S(1)}, u32[]{:S(2)}, u32[]{:S(2)}) async-start(bf16[16,5,7168]{2,1,0:T(8,128)(2,1)} %reshape.209), calls=%async_computation.7 | async-start | bytes 3670016 | tf_op jit(solution)/shard_map/all_to_all | solution.py:155
  635.4 0.1 pad_maximum_fusion
  635.5 1.1 copy.76
  636.6 0.1 fusion.57
  636.8 0.5 fusion.28
  637.3 1.1 pad_maximum_fusion.1
  638.3 23.0 %all-to-all-done.5 = bf16[16,5,7168]{2,1,0:T(8,128)(2,1)S(1)} async-done(((bf16[16,5,7168]{2,1,0:T(8,128)(2,1)}), bf16[16,5,7168]{2,1,0:T(8,128)(2,1)S(1)}, u32[]{:S(2)}, u32[]{:S(2)}) %all-to-all-start.5) | async-done | bytes 1146912 | tf_op jit(solution)/shard_map/all_to_all | solution.py:155
  661.3 0.6 reshape.210
  661.9 2.1 gather_fusion
  663.9 1.6 fusion.31
  665.6 0.7 fusion.56
  (68 shorter events, 0.9 us)
Async XLA Ops:
  7.2 123.8 %copy-start = (bf16[896,1152]{1,0:T(8,128)(2,1)S(1)}, bf16[896,1152]{1,0:T(8,128)(2,1)}, u32[]{:S(2)}) copy-start(bf16[896,1152]{1,0:T(8,128)(2,1)} %param.28) | copy-start | bytes 6193156
  7.2 202.9 %all-reduce.3.cloned.1.call-start = ((), (), s32[]{:S(2)}) async-start(), calls=%async_computation.11 | async-start | bytes 9437184 | tf_op jit(solution)/shard_map/psum | solution.py:109
  131.0 4.1 copy-start.16
  139.3 153.6 %reduce-scatter.3.cloned.1.call-start = ((), (), s32[]{:S(2)}) async-start(), calls=%async_computation.8 | async-start | bytes 1949696 | tf_op jit(solution)/shard_map/reduce_scatter | solution.py:113
  210.1 7.4 %copy-start.10 = (s32[8,8]{1,0:T(8,128)S(1)}, s32[8,8]{1,0:T(8,128)}, u32[]{:S(2)}) copy-start(s32[8,8]{1,0:T(8,128)} %param.34) | copy-start | bytes 772
  217.4 85.7 %copy-start.4 = (bf16[8,7168]{1,0:T(8,128)(2,1)S(1)}, bf16[8,7168]{1,0:T(8,128)(2,1)}, u32[]{:S(2)}) copy-start(bf16[8,7168]{1,0:T(8,128)(2,1)} %param.25) | copy-start | bytes 344068
  217.4 85.9 %copy-start.11 = (f32[7168]{0:T(1024)S(1)}, f32[7168]{0:T(1024)}, u32[]{:S(2)}) copy-start(f32[7168]{0:T(1024)} %param.30) | copy-start | bytes 86020
  292.9 10.2 %all-to-all-start.3 = ((bf16[8,8,896]{2,1,0:T(8,128)(2,1)}), bf16[8,8,896]{2,1,0:T(8,128)(2,1)S(1)}, u32[]{:S(2)}, u32[]{:S(2)}) async-start(bf16[8,8,896]{2,1,0:T(8,128)(2,1)} %bitcast.99), calls=%async_computation.4 | async-start | bytes 229376 | tf_op jit(solution)/shard_map/all_to_all | solution.py:119
  297.2 88.4 %all-gather.2.cloned.1.call-start = ((), (), s32[]{:S(2)}) async-start(), calls=%async_computation.9 | async-start | bytes 10321920 | tf_op jit(solution)/shard_map/all_gather | solution.py:142
  336.1 286.2 %reduce-scatter.5.cloned.1.call-start = ((), (), s32[]{:S(2)}) async-start(), calls=%async_computation.10 | async-start | bytes 10321920 | tf_op jit(solution)/shard_map/reduce_scatter | solution.py:148
  440.6 0.7 copy-start.13
  440.6 2.6 copy-start.3
  448.2 15.9 %copy-start.12 = (f32[8,8]{1,0:T(8,128)S(1)}, f32[8,8]{1,0:T(8,128)}, u32[]{:S(2)}) copy-start(f32[8,8]{1,0:T(8,128)} %param.35) | copy-start | bytes 772
  448.2 16.0 %copy-start.14 = (s32[128,2]{0,1:T(2,128)S(1)}, s32[128,2]{0,1:T(2,128)}, u32[]{:S(2)}) copy-start(s32[128,2]{0,1:T(2,128)} %param.23) | copy-start | bytes 3076
  448.2 18.0 %copy-start.15 = (s32[6]{0:T(128)S(1)}, s32[6]{0:T(128)}, u32[]{:S(2)}) copy-start(s32[6]{0:T(128)} %param.22) | copy-start | bytes 76
  448.2 18.1 %copy-start.9 = (bf16[8,576]{1,0:T(8,128)(2,1)S(1)}, bf16[8,576]{1,0:T(8,128)(2,1)}, u32[]{:S(2)}) copy-start(bf16[8,576]{1,0:T(8,128)(2,1)} %param.19) | copy-start | bytes 27652
  448.2 18.1 %copy-start.2 = (bf16[8,128,576]{1,2,0:T(8,128)(2,1)S(1)}, bf16[8,128,576]{1,2,0:T(8,128)(2,1)}, u32[]{:S(2)}) copy-start(bf16[8,128,576]{1,2,0:T(8,128)(2,1)} %param.18) | copy-start | bytes 3538948
  448.2 171.5 %all-to-all-start = ((bf16[16,2,256,576]{2,3,1,0:T(8,128)(2,1)}), bf16[16,2,256,576]{2,3,1,0:T(8,128)(2,1)}, u32[]{:S(2)}, u32[]{:S(2)}) async-start(bf16[16,2,256,576]{2,3,1,0:T(8,128)(2,1)} %select_select_fusion), calls=%async_computation | async-start | bytes 18874368 | tf_op jit(solution)/shard_map/all_to_all | solution.py:75
  466.5 2.9 copy-start.17
  621.2 3.7 copy-start.6
  624.9 36.4 %all-to-all-start.5 = ((bf16[16,5,7168]{2,1,0:T(8,128)(2,1)}), bf16[16,5,7168]{2,1,0:T(8,128)(2,1)S(1)}, u32[]{:S(2)}, u32[]{:S(2)}) async-start(bf16[16,5,7168]{2,1,0:T(8,128)(2,1)} %reshape.209), calls=%async_computation.7 | async-start | bytes 3670016 | tf_op jit(solution)/shard_map/all_to_all | solution.py:155
  635.4 1.2 copy-start.8
  635.4 1.4 copy-start.7
  635.5 1.8 copy-start.5
  661.9 4.4 copy-start.1
Sparse Core Ops, SparseCore 0:
  139.4 70.6 all-reduce.2
  217.5 75.3 reduce-scatter.2
  336.2 49.2 all-gather.1
  440.8 56.3 reduce-scatter.4
